TPU v7x, 32 devices: a whole 2x2x4 slice. The times are simulated.
32 devices in a mesh: rep: 2 (over y), grp: 8 (over z, x), sub: 2 (over core).
Axes of the slice: x: 2, y: 2, z: 4, core: 2. Of those that a mesh axis runs over, the one named last changes fastest.
Arguments:
- query_rows: bfloat16 [16, 4, 5120], P(('grp', 'sub'), 'rep'), parts along dimension 1, may hold values from -120 to 120
- cache_keys: bfloat16 [16, 4, 128, 1024], P(('grp', 'sub'), 'rep'), parts along dimension 1, may hold values from -6 to 6
- cache_values: bfloat16 [16, 4, 128, 1024], P(('grp', 'sub'), 'rep'), parts along dimension 1, may hold values from -6 to 6
- residual: bfloat16 [16, 4, 5120], P(('grp', 'sub'), 'rep'), parts along dimension 1, may hold values from -6 to 6
- lengths: int32 [16, 4], P(('grp', 'sub'), 'rep'), parts along dimension 1, may hold values from 3 to 128
- expert_ids: int32 [16, 4, 1], P(('grp', 'sub'), 'rep'), parts along dimension 1, may hold values from 0 to 3; in each aligned block of 2 rows (0 to 1, 2 to 3, ..., all dimensions but the last counted through in order) at most 2 rows name the same one
- capacity: int32 [4], replicated, may hold values from 1 to 2
- norm_gain: float32 [5120], replicated, may hold values from 0.5 to 1.5
- router: bfloat16 [5120, 4], replicated, may hold values from -0.078125 to 0.078125
- shared_gate: bfloat16 [5120, 8192], P(None, ('grp', 'sub')), may hold values from -0.078125 to 0.078125
- shared_up: bfloat16 [5120, 8192], P(None, ('grp', 'sub')), may hold values from -0.078125 to 0.078125
- shared_down: bfloat16 [8192, 5120], P(('grp', 'sub')), may hold values from -0.0625 to 0.0625
- expert_gate: bfloat16 [5120, 32768], P(None, ('grp', 'sub')), may hold values from -0.078125 to 0.078125
- expert_up: bfloat16 [5120, 32768], P(None, ('grp', 'sub')), may hold values from -0.078125 to 0.078125
- expert_down: bfloat16 [32768, 5120], P(('grp', 'sub')), may hold values from -0.0625 to 0.0625
Outputs:
- layer_out: bfloat16 [16, 4, 5120], P(('grp', 'sub'), 'rep'), parts along dimension 1
There are 2 independent parts, one for each index of `rep`. A program takes and returns all parts, laid end to end along the dimension named above; an argument that names none is the same for every part. Nothing has to cross between parts.
Inputs may be any that keep to these rules, and one draw needn't show every extreme that they name: `expert_ids`: in each aligned block of 2 rows (the rows of one device), no expert is named more than 2 times.
All inputs are finite; a program needn't handle non-finite values.
Results may differ from a plain program's by a relative error of at most 0.0075.
Values may be sent and summed in bfloat16 or wider, within the bound.
A program may use at most 128 MiB of HBM per device.

v0:
```python
import jax
import jax.numpy as jnp
from jax import lax
from jax.sharding import PartitionSpec as P

D = 5120
HEADS = 40
KV_HEADS = 8
HEAD = 128
EXPERTS = 4
EH = 8192


def attend(query_rows, cache_keys, cache_values, lengths):
    request_count = query_rows.shape[0]
    context = cache_keys.shape[1]
    groups = HEADS // KV_HEADS
    queries_f = query_rows.astype(jnp.float32).reshape(request_count, KV_HEADS, groups, HEAD)
    keys_f = cache_keys.astype(jnp.float32).reshape(request_count, context, KV_HEADS, HEAD)
    scores = jnp.einsum("rkgh,rjkh->rkgj", queries_f, keys_f) * HEAD ** (-0.5)
    key_pos = jnp.arange(context, dtype=jnp.int32)
    allowed = (key_pos[None, :] < lengths[:, None])[:, None, None, :]
    scores = jnp.where(allowed, scores, -1e30)
    row_peak = jnp.max(scores, axis=-1, keepdims=True)
    exponent = jnp.where(allowed, jnp.exp(scores - row_peak), 0.0)
    weights = (exponent / jnp.sum(exponent, axis=-1, keepdims=True)).astype(jnp.bfloat16)
    values_f = cache_values.astype(jnp.float32).reshape(request_count, context, KV_HEADS, HEAD)
    attended = jnp.einsum("rkgj,rjkh->rkgh", weights.astype(jnp.float32), values_f)
    return attended.reshape(request_count, HEADS * HEAD).astype(jnp.bfloat16)


def rms_normalize(stream, norm_gain):
    mean_square = jnp.mean(stream * stream, axis=-1, keepdims=True)
    return (stream * lax.rsqrt(mean_square + 1e-05) * norm_gain).astype(jnp.bfloat16)


def swiglu(inputs, w_gate, w_up, w_down):
    gate_part = jnp.dot(inputs, w_gate, preferred_element_type=jnp.float32)
    up_part = jnp.dot(inputs, w_up, preferred_element_type=jnp.float32)
    hidden = (jax.nn.silu(gate_part) * up_part).astype(jnp.bfloat16)
    return jnp.dot(hidden, w_down, preferred_element_type=jnp.float32)


def gated_inputs(flat_rows, router, route_ids):
    logits = jnp.dot(flat_rows, router, preferred_element_type=jnp.float32)
    onehot = route_ids[:, None] == jnp.arange(EXPERTS, dtype=jnp.int32)[None, :]
    picked = jnp.sum(jnp.where(onehot, logits, 0.0), axis=-1)
    return (flat_rows.astype(jnp.float32) * jax.nn.sigmoid(picked)[:, None]).astype(jnp.bfloat16)


def row_ranks(route_ids, capacity):
    onehot = (route_ids[:, None] == jnp.arange(EXPERTS, dtype=jnp.int32)[None, :]).astype(jnp.int32)
    before = jnp.cumsum(onehot, axis=0) - onehot
    row_rank = jnp.sum(before * onehot, axis=1)
    row_limit = jnp.sum(onehot * capacity[None, :], axis=1)
    return (row_rank, row_rank < row_limit)


def per_device(
    query_rows,
    cache_keys,
    cache_values,
    residual,
    lengths,
    expert_ids,
    capacity,
    norm_gain,
    router,
    shared_gate,
    shared_up,
    shared_down,
    expert_gate,
    expert_up,
    expert_down,
):
    tok_count = query_rows.shape[1]
    attended = attend(query_rows[0], cache_keys[0], cache_values[0], lengths[0])
    stream = residual[0].astype(jnp.float32) + attended.astype(jnp.float32)
    flat_rows = rms_normalize(stream, norm_gain)
    route_ids = expert_ids[0].reshape(tok_count)
    gathered, all_ids = (
        lax.all_gather(flat_rows, ("grp", "sub"), axis=0, tiled=True),
        lax.all_gather(route_ids, ("grp", "sub"), axis=0, tiled=True),
    )
    all_scaled = gated_inputs(gathered, router, all_ids)
    rank_unused, kept_all = jax.vmap(row_ranks, in_axes=(0, None))(
        all_ids.reshape(-1, tok_count), capacity
    )
    own_expert = lax.axis_index(("grp", "sub")) * expert_gate.shape[1] // EH
    usable = (all_ids == own_expert) & kept_all.reshape(-1)
    masked = jnp.where(usable[:, None], all_scaled, jnp.zeros_like(all_scaled))
    shared_part = swiglu(gathered, shared_gate, shared_up, shared_down)
    branch_sum = lax.psum_scatter(
        shared_part + swiglu(masked, expert_gate, expert_up, expert_down),
        ("grp", "sub"),
        scatter_dimension=0,
        tiled=True,
    )
    layer_out = stream + branch_sum
    return layer_out.astype(jnp.bfloat16).reshape(1, tok_count, D)


def solution(mesh):
    placed = (
        P(("grp", "sub"), "rep", None),
        P(("grp", "sub"), "rep", None, None),
        P(("grp", "sub"), "rep", None, None),
        P(("grp", "sub"), "rep", None),
        P(("grp", "sub"), "rep"),
        P(("grp", "sub"), "rep", None),
        P(),
        P(),
        P(),
        P(None, ("grp", "sub")),
        P(None, ("grp", "sub")),
        P(("grp", "sub"), None),
        P(None, ("grp", "sub")),
        P(None, ("grp", "sub")),
        P(("grp", "sub"), None),
    )
    return jax.shard_map(
        per_device,
        mesh=mesh,
        in_specs=placed,
        out_specs=P(("grp", "sub"), "rep", None),
        check_vma=False,
    )
```

profile of v0, /device:TPU:0, one launch (start us, length us, event | category | flops | bytes accessed | tf_op | source)
XLA Modules:
  0.0 184.4 jit_solution(740923644199911297)
XLA Ops:
  6.5 1.4 fusion.38
  8.6 0.8 bitcast_dynamic-update-slice_fusion
  9.4 13.7 %all-reduce = s32[32]{0:T(128)S(1)} all-reduce(s32[32]{0:T(128)S(1)} %bitcast_dynamic-update-slice_fusion), channel_id=2, replica_groups=mesh['rep'=2,'grp'=8,'sub'=2] {'grp','sub'}, use_global_device_ids=true, to_apply=%add | all-reduce | flops 32 | bytes 256 | tf_op jit(solution)/shard_map/all_gather | solution.py:83
  23.3 0.7 select_reduce_fusion
  24.1 0.1 copy.25
  24.2 0.1 lt.31
  24.3 0.7 iota_compare_fusion.3
  25.0 1.1 copy.26
  26.1 0.8 reshape.66
  26.9 0.4 fusion.5
  27.3 0.2 fusion.39
  27.5 1.1 copy.27
  28.6 0.3 fusion.7
  29.0 0.9 multiply_reduce_fusion
  29.9 0.8 fusion.29
  30.7 18.8 %all-gather.1 = bf16[16,2,5120]{2,1,0:T(2,128)(2,1)S(1)} all-gather(bf16[1,2,5120]{2,1,0:T(2,128)(2,1)S(1)} %fusion.29), channel_id=1, replica_groups=mesh['rep'=2,'grp'=8,'sub'=2] {'grp','sub'}, dimensions={0}, use_global_device_ids=true | all-gather | bytes 348160 | tf_op jit(solution)/shard_map/all_gather | solution.py:82
  49.6 0.1 reshape.78
  49.7 0.2 fusion.9
  49.9 3.5 %fusion.41 = f32[32,512]{1,0:T(8,128)S(1)} fusion(bf16[32,5120]{1,0:T(8,128)(2,1)S(1)} %reshape.78, bf16[5120,512]{1,0:T(8,128)(2,1)} %param.24), kind=kOutput, calls=%fused_computation.59 | convolution fusion | flops 167772160 | bytes 5636096 | tf_op jit(solution)/shard_map/dot_general | solution.py:38
  53.4 8.9 %fusion.36 = f32[32,2048]{1,0:T(8,128)S(1)} fusion(bf16[5120,2048]{1,0:T(8,128)(2,1)} %param.27, bf16[32,5120]{1,0:T(8,128)(2,1)S(1)} %reshape.78, f32[32]{0:T(128)S(1)} %add_divide_fusion, pred[32]{0:T(512)(128)(4,1)S(1)} %compare_and_fusion), kind=kOutput, calls=%fused_computation.55 | convolution fusion | flops 671744000 | bytes 21561504 | tf_op jit(solution)/shard_map/dot_general | solution.py:38
  62.4 16.8 %fusion.10 = f32[32,5120]{1,0:T(8,128)S(1)} fusion(bf16[2048,5120]{1,0:T(8,128)(2,1)} %param.29, bf16[5120,2048]{1,0:T(8,128)(2,1)} %param.28, f32[32,2048]{1,0:T(8,128)S(1)} %fusion.36, bf16[32,5120]{1,0:T(8,128)(2,1)S(1)} %reshape.78, f32[32]{0:T(128)S(1)} %add_divide_fusion, pred[32]{0:T(512)(128)(4,1)S(1)} %compare_and_fusion), kind=kOutput, calls=%fused_computation.18 | convolution fusion | flops 1343225856 | bytes 43188384 | tf_op jit(solution)/shard_map/dot_general | solution.py:41
  79.2 6.9 %convolution_add_fusion = f32[32,5120]{1,0:T(8,128)} fusion(f32[32,5120]{1,0:T(8,128)S(1)} %fusion.10, bf16[512,5120]{1,0:T(8,128)(2,1)} %param.26, bf16[32,5120]{1,0:T(8,128)(2,1)S(1)} %reshape.78, bf16[5120,512]{1,0:T(8,128)(2,1)} %param.25, f32[32,512]{1,0:T(8,128)S(1)} %fusion.41), kind=kOutput, calls=%fused_computation.1 | convolution fusion | flops 335806464 | bytes 12189696 | tf_op jit(solution)/shard_map/dot_general | solution.py:41
  86.8 89.3 %all-reduce.4.cloned.1.call-done = f32[32,5120]{1,0:T(8,128)} async-done(((f32[32,5120]{1,0:T(8,128)}), f32[32,5120]{1,0:T(8,128)}) %all-reduce.4.cloned.1.call-update) | async-done | bytes 655376
  176.0 1.6 fusion.28
  (17 shorter events, 0.3 us)
Async XLA Ops:
  6.5 43.2 %copy-start = (bf16[5120,4]{0,1:T(4,128)(2,1)S(1)}, bf16[5120,4]{0,1:T(4,128)(2,1)}, u32[]{:S(2)}) copy-start(bf16[5120,4]{0,1:T(4,128)(2,1)} %param.23) | copy-start | bytes 122884
  6.5 169.5 %all-reduce.4.cloned.1.call-start = ((), (), s32[]{:S(2)}) async-start(), calls=%async_computation | async-start | bytes 1310720
  62.4 113.6 %copy-start.2 = (bf16[1,2,5120]{2,1,0:T(2,128)(2,1)S(1)}, bf16[1,2,5120]{2,1,0:T(2,128)(2,1)}, u32[]{:S(2)}) copy-start(bf16[1,2,5120]{2,1,0:T(2,128)(2,1)} %param.18) | copy-start | bytes 61444
  62.4 115.2 %copy-start.1 = (bf16[5120,4]{0,1:T(4,128)(2,1)S(1)}, bf16[5120,4]{0,1:T(4,128)(2,1)}, u32[]{:S(2)}) copy-start(bf16[5120,4]{0,1:T(4,128)(2,1)} %param.23) | copy-start | bytes 122884
Sparse Core Ops, SparseCore 0:
  86.2 89.7 all-reduce.3
where the time goes:
time: 185 us; the launch traced here: 184 us
  waiting for transfers between devices  89.3 us (48%)
  matrix products  37 us (20%)
  blocking collectives  32.6 us (18%)
  between operations  14.8 us (8%)
  local copies, waits for them, and re-layouts  5.71 us (3%)
  other arithmetic  5.03 us (3%)
    unnamed x2, waiting for transfers between devices  89.3 us
    dot_general x2, matrix products, swiglu(): return jnp.dot(hidden, w_down, preferred_element_type=jnp.float32)  23.7 us
    all_gather x1, blocking collectives, per_device(): lax.all_gather(flat_rows, ('grp', 'sub'), axis=0, tiled=True)  18.8 us
    all_gather x1, blocking collectives, per_device(): lax.all_gather(route_ids, ('grp', 'sub'), axis=0, tiled=True)  13.7 us
    dot_general x2, matrix products, swiglu(): gate_part = jnp.dot(inputs, w_gate, preferred_element_type=jnp.float32)  12.4 us
    unnamed x12, local copies, waits for them, and re-layouts  4.56 us
  transfers between devices with their start and end apart: 1, of which 1 were waited for; matrix products, arithmetic and copies ran while one was open for 0% of the time, Pallas kernels for 0%

commit v1 on v0

--- a/solution.py
+++ b/solution.py
@@ -9,6 +9,13 @@
 HEAD = 128
 EXPERTS = 4
 EH = 8192
+
+
+def all_by_exchange(x, axis, dim):
+    count = lax.axis_size(axis)
+    parts = jnp.stack([x for _ in range(count)])
+    parts = lax.all_to_all(parts, axis, split_axis=0, concat_axis=0)
+    return jnp.concatenate(parts, axis=dim)
 
 
 def attend(query_rows, cache_keys, cache_values, lengths):
@@ -79,7 +86,7 @@
     flat_rows = rms_normalize(stream, norm_gain)
     route_ids = expert_ids[0].reshape(tok_count)
     gathered, all_ids = (
-        lax.all_gather(flat_rows, ("grp", "sub"), axis=0, tiled=True),
+        all_by_exchange(flat_rows, ("grp", "sub"), 0),
         lax.all_gather(route_ids, ("grp", "sub"), axis=0, tiled=True),
     )
     all_scaled = gated_inputs(gathered, router, all_ids)

time: 185 us -> 173 us (0.935)
  blocking collectives: 32.6 us -> 12.4 us
  starting transfers between devices: 0.01 us -> 7.43 us
    all_gather x1 -> x0, blocking collectives: 18.8 us -> none  [per_device(): lax.all_gather(flat_rows, ('grp', 'sub'), axis=0, tiled=True)]
    all_to_all x0 -> x1, starting transfers between devices: none -> 7.39 us  [all_by_exchange(): parts = lax.all_to_all(parts, axis, split_axis=0, concat_axis=0)]
    unnamed x12 -> x11, local copies, waits for them, and re-layouts: 4.56 us -> 4.44 us
  transfers between devices with their start and end apart: 1 -> 2, of which waited for: 1 -> 1; matrix products, arithmetic and copies ran while one was open for 0% -> 2% of each run, Pallas kernels for 0% -> 0%
where the time goes in v1:
time: 173 us; the launch traced here: 172 us
  waiting for transfers between devices  88.9 us (51%)
  matrix products  37 us (21%)
  between operations  14.9 us (9%)
  blocking collectives  12.4 us (7%)
  starting transfers between devices  7.43 us (4%)
  local copies, waits for them, and re-layouts  6.63 us (4%)
  other arithmetic  5.03 us (3%)
    unnamed x2, waiting for transfers between devices  88.9 us
    dot_general x2, matrix products, swiglu(): return jnp.dot(hidden, w_down, preferred_element_type=jnp.float32)  23.7 us
    dot_general x2, matrix products, swiglu(): gate_part = jnp.dot(inputs, w_gate, preferred_element_type=jnp.float32)  12.4 us
    all_gather x1, blocking collectives, per_device(): lax.all_gather(route_ids, ('grp', 'sub'), axis=0, tiled=True)  12.4 us
    all_to_all x1, starting transfers between devices, all_by_exchange(): parts = lax.all_to_all(parts, axis, split_axis=0, concat_axis=0)  7.39 us
    unnamed x11, local copies, waits for them, and re-layouts  4.44 us
  transfers between devices with their start and end apart: 2, of which 1 were waited for; matrix products, arithmetic and copies ran while one was open for 2% of the time, Pallas kernels for 0%

profile of v1, /device:TPU:0, one launch (start us, length us, event | category | flops | bytes accessed | tf_op | source)
XLA Modules:
  0.0 172.3 jit_solution(8611515049066876271)
XLA Ops:
  6.5 0.7 iota_compare_fusion.3
  7.3 1.1 copy.26
  8.4 0.8 reshape.99
  9.2 0.4 fusion.5
  9.5 0.2 fusion.43
  9.7 1.1 copy.27
  10.9 0.3 fusion.7
  11.3 0.9 multiply_reduce_fusion
  12.2 0.8 fusion.33
  13.0 0.9 stack.5
  13.9 7.4 %all-to-all-start = ((bf16[16,2,5120]{2,1,0:T(2,128)(2,1)}), bf16[16,2,5120]{2,1,0:T(2,128)(2,1)S(1)}, u32[]{:S(2)}, u32[]{:S(2)}) async-start(bf16[16,2,5120]{2,1,0:T(2,128)(2,1)} %stack.5), calls=%async_computation | async-start | bytes 655360 | tf_op jit(solution)/shard_map/all_to_all | solution.py:17
  21.3 1.4 fusion.42
  23.5 0.8 bitcast_dynamic-update-slice_fusion
  24.2 12.4 %all-reduce = s32[32]{0:T(128)S(1)} all-reduce(s32[32]{0:T(128)S(1)} %bitcast_dynamic-update-slice_fusion), channel_id=2, replica_groups=mesh['rep'=2,'grp'=8,'sub'=2] {'grp','sub'}, use_global_device_ids=true, to_apply=%add | all-reduce | flops 32 | bytes 256 | tf_op jit(solution)/shard_map/all_gather | solution.py:90
  36.7 0.8 select_reduce_fusion
  37.5 0.1 copy.25
  37.8 0.1 reshape.102
  37.9 0.2 fusion.9
  38.1 3.5 %fusion.45 = f32[32,512]{1,0:T(8,128)S(1)} fusion(bf16[32,5120]{1,0:T(8,128)(2,1)S(1)} %reshape.102, bf16[5120,512]{1,0:T(8,128)(2,1)} %param.24), kind=kOutput, calls=%fused_computation.63 | convolution fusion | flops 167772160 | bytes 5636096 | tf_op jit(solution)/shard_map/dot_general | solution.py:45
  41.6 8.9 %fusion.40 = f32[32,2048]{1,0:T(8,128)S(1)} fusion(bf16[5120,2048]{1,0:T(8,128)(2,1)} %param.27, bf16[32,5120]{1,0:T(8,128)(2,1)S(1)} %reshape.102, f32[32]{0:T(128)S(1)} %add_divide_fusion, pred[32]{0:T(512)(128)(4,1)S(1)} %compare_and_fusion), kind=kOutput, calls=%fused_computation.59 | convolution fusion | flops 671744000 | bytes 21561504 | tf_op jit(solution)/shard_map/dot_general | solution.py:45
  50.6 16.8 %fusion.10 = f32[32,5120]{1,0:T(8,128)S(1)} fusion(bf16[2048,5120]{1,0:T(8,128)(2,1)} %param.29, bf16[5120,2048]{1,0:T(8,128)(2,1)} %param.28, f32[32,2048]{1,0:T(8,128)S(1)} %fusion.40, bf16[32,5120]{1,0:T(8,128)(2,1)S(1)} %reshape.102, f32[32]{0:T(128)S(1)} %add_divide_fusion, pred[32]{0:T(512)(128)(4,1)S(1)} %compare_and_fusion), kind=kOutput, calls=%fused_computation.18 | convolution fusion | flops 1343225856 | bytes 43188384 | tf_op jit(solution)/shard_map/dot_general | solution.py:48
  67.4 6.9 %convolution_add_fusion = f32[32,5120]{1,0:T(8,128)} fusion(f32[32,5120]{1,0:T(8,128)S(1)} %fusion.10, bf16[512,5120]{1,0:T(8,128)(2,1)} %param.26, bf16[32,5120]{1,0:T(8,128)(2,1)S(1)} %reshape.102, bf16[5120,512]{1,0:T(8,128)(2,1)} %param.25, f32[32,512]{1,0:T(8,128)S(1)} %fusion.45), kind=kOutput, calls=%fused_computation.1 | convolution fusion | flops 335806464 | bytes 12189696 | tf_op jit(solution)/shard_map/dot_general | solution.py:48
  74.9 88.9 %all-reduce.4.cloned.1.call-done = f32[32,5120]{1,0:T(8,128)} async-done(((f32[32,5120]{1,0:T(8,128)}), f32[32,5120]{1,0:T(8,128)}) %all-reduce.4.cloned.1.call-update) | async-done | bytes 655376
  163.9 1.6 fusion.32
  (20 shorter events, 0.5 us)
Async XLA Ops:
  6.5 31.4 %copy-start = (bf16[5120,4]{0,1:T(4,128)(2,1)S(1)}, bf16[5120,4]{0,1:T(4,128)(2,1)}, u32[]{:S(2)}) copy-start(bf16[5120,4]{0,1:T(4,128)(2,1)} %param.23) | copy-start | bytes 122884
  13.9 23.9 %all-to-all-start = ((bf16[16,2,5120]{2,1,0:T(2,128)(2,1)}), bf16[16,2,5120]{2,1,0:T(2,128)(2,1)S(1)}, u32[]{:S(2)}, u32[]{:S(2)}) async-start(bf16[16,2,5120]{2,1,0:T(2,128)(2,1)} %stack.5), calls=%async_computation | async-start | bytes 655360 | tf_op jit(solution)/shard_map/all_to_all | solution.py:17
  21.3 142.6 %all-reduce.4.cloned.1.call-start = ((), (), s32[]{:S(2)}) async-start(), calls=%async_computation.1 | async-start | bytes 1310720
  50.6 113.3 %copy-start.2 = (bf16[1,2,5120]{2,1,0:T(2,128)(2,1)S(1)}, bf16[1,2,5120]{2,1,0:T(2,128)(2,1)}, u32[]{:S(2)}) copy-start(bf16[1,2,5120]{2,1,0:T(2,128)(2,1)} %param.18) | copy-start | bytes 61444
  50.6 114.9 %copy-start.1 = (bf16[5120,4]{0,1:T(4,128)(2,1)S(1)}, bf16[5120,4]{0,1:T(4,128)(2,1)}, u32[]{:S(2)}) copy-start(bf16[5120,4]{0,1:T(4,128)(2,1)} %param.23) | copy-start | bytes 122884
Sparse Core Ops, SparseCore 0:
  74.4 89.3 all-reduce.3
